TPU v7x, 32 devices: a whole 2x2x4 slice. The times are simulated.
32 devices in a mesh: dp: 8 (over z, x), outer: 4 (over y, core).
Axes of the slice: x: 2, y: 2, z: 4, core: 2. Of those that a mesh axis runs over, the one named last changes fastest.
Arguments:
- partials: bfloat16 [4, 8, 2, 16, 8192], P('outer', 'dp'), may hold values from -3500 to 3500, as said below
- master: float32 [2, 16, 8192], P(None, 'dp'), may hold values from -6 to 6
- m_codes: bfloat16 [2, 16, 8192], P(None, 'dp'), may hold values from -1 to 1
- v_codes: bfloat16 [2, 16, 8192], P(None, 'dp'), may hold values from 0.049804688 to 1
- m_scales: float32 [2, 16, 4], P(None, 'dp'), may hold values from 0.0001 to 0.001
- v_scales: float32 [2, 16, 4], P(None, 'dp'), may hold values from 1e-08 to 1e-07
Outputs:
- new_master: float32 [2, 16, 8192], P(None, 'dp')
- new_m_codes: bfloat16 [2, 16, 8192], P(None, 'dp')
- new_v_codes: bfloat16 [2, 16, 8192], P(None, 'dp')
- new_m_scales: float32 [2, 16, 4], P(None, 'dp')
- new_v_scales: float32 [2, 16, 4], P(None, 'dp')
- weights: bfloat16 [2, 16, 8192], replicated
Inputs may be any that keep to these rules, and one draw needn't show every extreme that they name: Gradient partials of real values; entries vary from row to row and column to column.
All inputs are finite; a program needn't handle non-finite values. Where the computation divides by a largest or mean magnitude, that divisor is 1e-20 or more.
Results may differ from a plain program's by a relative error of at most 0.0004.
Values may be sent and summed in bfloat16 or wider, within the bound.
No kernel may reach another device: no remote copies, remote signals or barrier semaphores. Data moves between devices by JAX's collectives and lax.ppermute only.
A program may use at most 64 MiB of HBM per device.

v0:
```python
import jax
import jax.numpy as jnp
from jax import lax
from jax.sharding import PartitionSpec as P

BLOCK = 2048
STEP = 10


def adam_blocks(gradient, master, m_codes, v_codes, m_scales, v_scales, clip_factor):
    count = gradient.shape[0]
    rows = gradient.shape[1]
    blocks = gradient.shape[2] // BLOCK
    shape_four = (count, rows, blocks, BLOCK)
    moment = m_codes.astype(jnp.float32).reshape(shape_four) * m_scales[..., None]
    second = v_codes.astype(jnp.float32).reshape(shape_four) * v_scales[..., None]
    scaled = clip_factor * gradient.reshape(shape_four)
    moment = 0.9 * moment + 0.1 * scaled
    second = 0.95 * second + 0.05 * scaled * scaled
    update = moment / (1.0 - 0.9**STEP) / (jnp.sqrt(second / (1.0 - 0.95**STEP)) + 1e-08)
    fresh = master - 0.01 * update.reshape(master.shape)
    m_top = jnp.max(jnp.abs(moment), axis=3) + 1e-20
    v_top = jnp.max(jnp.abs(second), axis=3) + 1e-20
    m_next = (moment / m_top[..., None]).astype(jnp.bfloat16).reshape(master.shape)
    v_next = (second / v_top[..., None]).astype(jnp.bfloat16).reshape(master.shape)
    return (fresh, m_next, v_next, m_top, v_top, fresh.astype(jnp.bfloat16))


def body(partials, master, m_codes, v_codes, m_scales, v_scales):
    own_terms = partials[0, 0]
    row_part = lax.psum_scatter(
        own_terms.astype(jnp.float32), "dp", scatter_dimension=1, tiled=True
    )
    gradient = lax.psum(row_part, "outer")
    total = lax.psum(jnp.sum(gradient * gradient), "dp")
    clip_factor = 1.0 / jnp.maximum(jnp.sqrt(total), 1.0)
    results = adam_blocks(gradient, master, m_codes, v_codes, m_scales, v_scales, clip_factor)
    fresh, m_next, v_next, m_top, v_top, rounded = results
    weights = lax.all_gather(rounded, "dp", axis=1, tiled=True)
    return (fresh, m_next, v_next, m_top, v_top, weights)


def solution(mesh):
    return jax.shard_map(
        body,
        mesh=mesh,
        in_specs=(
            P("outer", "dp", None, None, None),
            P(None, "dp", None),
            P(None, "dp", None),
            P(None, "dp", None),
            P(None, "dp", None),
            P(None, "dp", None),
        ),
        out_specs=(
            P(None, "dp", None),
            P(None, "dp", None),
            P(None, "dp", None),
            P(None, "dp", None),
            P(None, "dp", None),
            P(),
        ),
        check_vma=False,
    )
```

profile of v0, /device:TPU:0, one launch (start us, length us, event | category | flops | bytes accessed | tf_op | source)
XLA Modules:
  0.0 194.2 jit_solution(15518864114638072132)
XLA Ops:
  7.2 0.0 all-reduce.6.cloned.1.call-start
  7.2 2.1 %bitcast_convert_fusion = f32[2,16,8192]{2,1,0:T(8,128)} fusion(bf16[1,1,2,16,8192]{4,3,2,1,0:T(8,128)(2,1)} %param.6), kind=kLoop, calls=%fused_computation | loop fusion | flops 262144 | bytes 1572864 | tf_op jit(solution)/shard_map/convert_element_type | solution.py:32
  9.3 0.0 all-reduce.6.cloned.1.call-update
  9.4 0.0 all-reduce.4.cloned.1.call-start
  9.4 0.0 copy-start.8
  9.4 0.6 copy-done.8
  10.1 0.6 dynamic-slice
  11.3 81.3 %all-reduce.6.cloned.1.call-done = f32[2,16,8192]{2,1,0:T(8,128)} async-done(((f32[2,16,8192]{2,1,0:T(8,128)}), f32[2,16,8192]{2,1,0:T(8,128)}) %all-reduce.6.cloned.1.call-update) | async-done | bytes 1048592
  92.6 1.7 constant_dynamic-slice_fusion
  94.3 0.0 copy-start.5
  94.3 0.0 all-reduce.4.cloned.1.call-update
  94.4 0.7 copy-done.5
  95.0 0.1 mul.104
  95.1 0.0 copy-start.4
  95.1 0.1 mul.105
  95.3 0.5 copy-done.4
  95.8 0.1 mul.114
  95.9 0.0 copy-start.1
  95.9 0.1 mul.115
  96.0 0.7 copy-done.1
  96.7 0.1 reshape.40
  96.8 0.0 copy-start
  96.8 30.1 %all-reduce.4.cloned.1.call-done = f32[2,2,8192]{2,1,0:T(2,128)} async-done(((f32[2,2,8192]{2,1,0:T(2,128)}), f32[2,2,8192]{2,1,0:T(2,128)}) %all-reduce.4.cloned.1.call-update) | async-done | bytes 131088 | tf_op jit(solution)/shard_map/psum | solution.py:34
  126.9 0.0 copy-start.3
  126.9 1.7 multiply_reduce_fusion
  128.6 0.0 copy-done
  128.6 0.0 copy-start.2
  128.6 0.1 reshape.41
  128.6 22.0 %psum.15 = f32[]{:T(128)} all-reduce(f32[]{:T(128)} %multiply_reduce_fusion), channel_id=1, replica_groups=mesh['dp'=8,'outer'=4] {'dp'}, use_global_device_ids=true, to_apply=%region_3.0 | all-reduce | flops 1 | bytes 8 | tf_op jit(solution)/shard_map/psum | solution.py:35
  151.4 0.0 copy-done.3
  151.4 0.0 copy-done.2
  151.4 1.1 fusion.4
  152.5 0.1 mul.127
  152.6 0.3 fusion.3
  152.9 0.0 copy-start.7
  152.9 0.0 copy-start.6
  152.9 0.1 div.47
  153.0 0.5 copy-done.7
  153.5 0.1 div.48
  153.6 0.0 copy-done.6
  153.6 0.1 div.50
  153.7 0.1 div.51
  153.9 0.1 copy.12
  153.9 31.4 %all_gather.3 = bf16[2,16,8192]{2,0,1:T(2,128)(2,1)S(1)} all-gather(bf16[2,2,8192]{2,0,1:T(2,128)(2,1)S(1)} %copy.12), channel_id=1, replica_groups=mesh['dp'=8,'outer'=4] {'dp'}, dimensions={1}, use_global_device_ids=true | all-gather | bytes 589824 | tf_op jit(solution)/shard_map/all_gather | solution.py:39
  185.3 1.1 copy.13
  186.4 1.0 divide_convert_fusion
  (1 shorter events, 0.0 us)
Async XLA Ops:
  7.2 85.4 %all-reduce.6.cloned.1.call-start = ((), (), s32[]{:S(2)}) async-start(), calls=%async_computation.1 | async-start | bytes 2097152
  9.4 117.5 %all-reduce.4.cloned.1.call-start = ((), (), s32[]{:S(2)}) async-start(), calls=%async_computation | async-start | bytes 262144 | tf_op jit(solution)/shard_map/psum | solution.py:34
  9.4 0.7 copy-start.8
  94.3 0.7 copy-start.5
  95.1 0.7 copy-start.4
  95.9 0.8 copy-start.1
  96.8 31.8 %copy-start = (bf16[2,2,8192]{2,1,0:T(2,128)(2,1)S(1)}, bf16[2,2,8192]{2,1,0:T(2,128)(2,1)}, u32[]{:S(2)}) copy-start(bf16[2,2,8192]{2,1,0:T(2,128)(2,1)} %param.9) | copy-start | bytes 196612
  126.9 24.5 %copy-start.3 = (f32[2,2,8192]{2,1,0:T(2,128)S(1)}, f32[2,2,8192]{2,1,0:T(2,128)}, u32[]{:S(2)}) copy-start(f32[2,2,8192]{2,1,0:T(2,128)} %param.7) | copy-start | bytes 393220
  128.6 22.8 %copy-start.2 = (f32[2,2,8192]{2,1,0:T(2,128)S(1)}, f32[2,2,8192]{2,1,0:T(2,128)}, u32[]{:S(2)}) copy-start(f32[2,2,8192]{2,1,0:T(2,128)} %all-reduce.4.cloned.1.call-done) | copy-start | bytes 393220
  152.9 0.6 copy-start.7
  152.9 0.7 copy-start.6
Sparse Core Ops, SparseCore 0:
  11.5 81.0 all-reduce.5
  95.5 31.3 all-reduce.3
where the time goes:
time: 195 us; the launch traced here: 194 us
  waiting for transfers between devices  111 us (57%)
  blocking collectives  53.4 us (27%)
  between operations  15.6 us (8%)
  local copies, waits for them, and re-layouts  7.63 us (4%)
  other arithmetic  6.17 us (3%)
    unnamed x3, waiting for transfers between devices  81.3 us
    all_gather x1, blocking collectives, body(): weights = lax.all_gather(rounded, 'dp', axis=1, tiled=True)  31.4 us
    psum x1, waiting for transfers between devices, body(): gradient = lax.psum(row_part, 'outer')  30.1 us
    psum x1, blocking collectives, body(): total = lax.psum(jnp.sum(gradient * gradient), 'dp')  22 us
    unnamed x21, local copies, waits for them, and re-layouts  6.46 us
  transfers between devices with their start and end apart: 2, of which 2 were waited for; matrix products, arithmetic and copies ran while one was open for 1% of the time, Pallas kernels for 0%

commit v1 on v0

--- a/solution.py
+++ b/solution.py
@@ -5,6 +5,12 @@
 
 BLOCK = 2048
 STEP = 10
+
+
+def gather_and_add(array, name):
+    terms = lax.all_gather(array, name, axis=0, tiled=False)
+    total = terms.sum(axis=0)
+    return total
 
 
 def adam_blocks(gradient, master, m_codes, v_codes, m_scales, v_scales, clip_factor):
@@ -31,7 +37,7 @@
     row_part = lax.psum_scatter(
         own_terms.astype(jnp.float32), "dp", scatter_dimension=1, tiled=True
     )
-    gradient = lax.psum(row_part, "outer")
+    gradient = gather_and_add(row_part, "outer")
     total = lax.psum(jnp.sum(gradient * gradient), "dp")
     clip_factor = 1.0 / jnp.maximum(jnp.sqrt(total), 1.0)
     results = adam_blocks(gradient, master, m_codes, v_codes, m_scales, v_scales, clip_factor)

time: 195 us -> 167 us (0.86)
  waiting for transfers between devices: 111 us -> 78.8 us
  blocking collectives: 53.4 us -> 59 us
    psum x1 -> x0, waiting for transfers between devices: 30.1 us -> none  [body(): gradient = lax.psum(row_part, 'outer')]
    all_gather x0 -> x1, blocking collectives: none -> 7.15 us  [gather_and_add(): terms = lax.all_gather(array, name, axis=0, tiled=False)]
    unnamed x3 -> x2, waiting for transfers between devices: 81.3 us -> 78.8 us
  transfers between devices with their start and end apart: 2 -> 1, of which waited for: 2 -> 1; matrix products, arithmetic and copies ran while one was open for 1% -> 1% of each run, Pallas kernels for 0% -> 0%
where the time goes in v1:
time: 167 us
  waiting for transfers between devices  78.8 us (47%)
  blocking collectives  59 us (35%)
  between operations  15.6 us (9%)
  local copies, waits for them, and re-layouts  7.58 us (5%)
  other arithmetic  5.72 us (3%)
    unnamed x2, waiting for transfers between devices  78.8 us
    all_gather x1, blocking collectives, body(): weights = lax.all_gather(rounded, 'dp', axis=1, tiled=True)  31.2 us
    psum x1, blocking collectives, body(): total = lax.psum(jnp.sum(gradient * gradient), 'dp')  20.7 us
    all_gather x1, blocking collectives, gather_and_add(): terms = lax.all_gather(array, name, axis=0, tiled=False)  7.15 us
    unnamed x21, local copies, waits for them, and re-layouts  6.4 us
  transfers between devices with their start and end apart: 1, of which 1 were waited for; matrix products, arithmetic and copies ran while one was open for 1% of the time, Pallas kernels for 0%

profile of v1, /device:TPU:0, one launch (start us, length us, event | category | flops | bytes accessed | tf_op | source)
XLA Modules:
  0.0 166.7 jit_solution(9270559959030567855)
XLA Ops:
  7.2 0.0 all-reduce.3.cloned.1.call-start
  7.2 2.1 %bitcast_convert_fusion = f32[2,16,8192]{2,1,0:T(8,128)} fusion(bf16[1,1,2,16,8192]{4,3,2,1,0:T(8,128)(2,1)} %param.6), kind=kLoop, calls=%fused_computation | loop fusion | flops 262144 | bytes 1572864 | tf_op jit(solution)/shard_map/convert_element_type | solution.py:38
  9.4 0.0 all-reduce.3.cloned.1.call-update
  9.4 0.0 copy-start.5
  9.4 0.7 copy-done.5
  10.1 0.1 mul.104
  10.2 0.0 copy-start.6
  10.2 0.1 reshape.47
  10.3 0.5 copy-done.6
  10.9 0.1 mul.114
  10.9 0.0 copy-start.1
  11.0 0.1 reshape.48
  11.1 0.7 copy-done.1
  11.8 0.1 reshape.40
  11.9 0.0 copy-start.7
  11.9 0.6 copy-done.7
  12.5 0.6 dynamic-slice
  13.7 78.7 %all-reduce.3.cloned.1.call-done = f32[2,16,8192]{2,1,0:T(8,128)} async-done(((f32[2,16,8192]{2,1,0:T(8,128)}), f32[2,16,8192]{2,1,0:T(8,128)}) %all-reduce.3.cloned.1.call-update) | async-done | bytes 1048592
  92.5 1.1 constant_dynamic-slice_fusion
  93.6 7.2 %all-gather = f32[8,2,8192]{2,1,0:T(2,128)S(1)} all-gather(f32[2,2,8192]{2,1,0:T(2,128)S(1)} %constant_dynamic-slice_fusion), channel_id=2, replica_groups=mesh['dp'=8,'outer'=4] {'outer'}, dimensions={0}, use_global_device_ids=true | all-gather | bytes 655360 | tf_op jit(solution)/shard_map/all_gather | solution.py:11
  100.7 0.3 reduce_sum.18
  101.0 0.0 copy-start
  101.0 0.7 multiply_reduce_fusion
  101.8 0.1 copy-done
  101.9 0.0 copy-start.2
  101.9 0.1 reshape.41
  101.9 20.7 %psum.7 = f32[]{:T(128)} all-reduce(f32[]{:T(128)} %multiply_reduce_fusion), channel_id=1, replica_groups=mesh['dp'=8,'outer'=4] {'dp'}, use_global_device_ids=true, to_apply=%region_3.0 | all-reduce | flops 1 | bytes 8 | tf_op jit(solution)/shard_map/psum | solution.py:41
  123.4 0.0 copy-done.2
  123.4 1.2 fusion.12
  124.6 0.1 mul.127
  124.7 0.3 fusion.3
  125.0 0.0 copy-start.3
  125.0 0.1 div.47
  125.1 0.5 copy-done.3
  125.6 0.1 div.48
  125.7 0.0 copy-start.4
  125.7 0.1 div.50
  125.8 0.5 copy-done.4
  126.3 0.1 div.51
  126.4 0.1 copy.34
  126.5 31.2 %all_gather.11 = bf16[2,16,8192]{2,0,1:T(2,128)(2,1)S(1)} all-gather(bf16[2,2,8192]{2,0,1:T(2,128)(2,1)S(1)} %copy.34), channel_id=1, replica_groups=mesh['dp'=8,'outer'=4] {'dp'}, dimensions={1}, use_global_device_ids=true | all-gather | bytes 589824 | tf_op jit(solution)/shard_map/all_gather | solution.py:45
  157.7 1.1 copy.37
  158.8 1.1 divide_convert_fusion
  (5 shorter events, 0.0 us)
Async XLA Ops:
  7.2 85.3 %all-reduce.3.cloned.1.call-start = ((), (), s32[]{:S(2)}) async-start(), calls=%async_computation | async-start | bytes 2097152
  9.4 0.7 copy-start.5
  10.2 0.7 copy-start.6
  10.9 0.8 copy-start.1
  11.9 0.7 copy-start.7
  101.0 0.8 copy-start
  101.9 21.5 %copy-start.2 = (f32[2,2,8192]{2,1,0:T(2,128)S(1)}, f32[2,2,8192]{2,1,0:T(2,128)}, u32[]{:S(2)}) copy-start(f32[2,2,8192]{2,1,0:T(2,128)} %param.7) | copy-start | bytes 393220
  125.0 0.6 copy-start.3
  125.7 0.6 copy-start.4
Sparse Core Ops, SparseCore 0:
  11.5 80.9 all-reduce.2

commit v2 on v0

--- a/solution.py
+++ b/solution.py
@@ -36,7 +36,12 @@
     clip_factor = 1.0 / jnp.maximum(jnp.sqrt(total), 1.0)
     results = adam_blocks(gradient, master, m_codes, v_codes, m_scales, v_scales, clip_factor)
     fresh, m_next, v_next, m_top, v_top, rounded = results
-    weights = lax.all_gather(rounded, "dp", axis=1, tiled=True)
+    weights = jnp.concatenate(
+        lax.all_to_all(
+            jnp.stack([rounded for _ in range(lax.axis_size("dp"))], axis=0), "dp", 0, 0
+        ),
+        axis=1,
+    )
     return (fresh, m_next, v_next, m_top, v_top, weights)
 
 

time: 195 us -> 178 us (0.913)
  blocking collectives: 53.4 us -> 22 us
  waiting for transfers between devices: 111 us -> 121 us
  starting transfers between devices: 0.08 us -> 3.57 us
    all_gather x1 -> x0, blocking collectives: 31.4 us -> none  [body(): weights = lax.all_gather(rounded, 'dp', axis=1, tiled=True)]
    all_to_all x0 -> x1, waiting for transfers between devices: none -> 9.25 us  [body(): lax.all_to_all(jnp.stack([rounded for _ in range(lax.axis_size('dp'))], a...]
    all_to_all x0 -> x1, starting transfers between devices: none -> 3.49 us  [body(): lax.all_to_all(jnp.stack([rounded for _ in range(lax.axis_size('dp'))], a...]
  transfers between devices with their start and end apart: 2 -> 3, of which waited for: 2 -> 3; matrix products, arithmetic and copies ran while one was open for 1% -> 1% of each run, Pallas kernels for 0% -> 0%
where the time goes in v2:
time: 178 us; the launch traced here: 177 us
  waiting for transfers between devices  121 us (68%)
  blocking collectives  22 us (12%)
  between operations  15.6 us (9%)
  local copies, waits for them, and re-layouts  9.3 us (5%)
  other arithmetic  6.16 us (3%)
  starting transfers between devices  3.57 us (2%)
    unnamed x3, waiting for transfers between devices  81.3 us
    psum x1, waiting for transfers between devices, body(): gradient = lax.psum(row_part, 'outer')  30.1 us
    psum x1, blocking collectives, body(): total = lax.psum(jnp.sum(gradient * gradient), 'dp')  22 us
    all_to_all x1, waiting for transfers between devices, body(): lax.all_to_all(jnp.stack([rounded for _ in range(lax.axis_size('dp'))], a...  9.25 us
    unnamed x21, local copies, waits for them, and re-layouts  6.46 us
  transfers between devices with their start and end apart: 3, of which 3 were waited for; matrix products, arithmetic and copies ran while one was open for 1% of the time, Pallas kernels for 0%

profile of v2, /device:TPU:0, one launch (start us, length us, event | category | flops | bytes accessed | tf_op | source)
XLA Modules:
  0.0 177.2 jit_solution(13179929107595635660)
XLA Ops:
  7.2 0.0 all-reduce.6.cloned.1.call-start
  7.2 2.1 %bitcast_convert_fusion = f32[2,16,8192]{2,1,0:T(8,128)} fusion(bf16[1,1,2,16,8192]{4,3,2,1,0:T(8,128)(2,1)} %param.6), kind=kLoop, calls=%fused_computation | loop fusion | flops 262144 | bytes 1572864 | tf_op jit(solution)/shard_map/convert_element_type | solution.py:32
  9.3 0.0 all-reduce.6.cloned.1.call-update
  9.4 0.0 all-reduce.4.cloned.1.call-start
  9.4 0.0 copy-start.8
  9.4 0.6 copy-done.8
  10.1 0.6 dynamic-slice
  11.3 81.3 %all-reduce.6.cloned.1.call-done = f32[2,16,8192]{2,1,0:T(8,128)} async-done(((f32[2,16,8192]{2,1,0:T(8,128)}), f32[2,16,8192]{2,1,0:T(8,128)}) %all-reduce.6.cloned.1.call-update) | async-done | bytes 1048592
  92.6 1.7 constant_dynamic-slice_fusion
  94.3 0.0 copy-start.5
  94.3 0.0 all-reduce.4.cloned.1.call-update
  94.4 0.7 copy-done.5
  95.0 0.1 mul.104
  95.1 0.0 copy-start.4
  95.1 0.1 mul.105
  95.3 0.5 copy-done.4
  95.8 0.1 mul.114
  95.9 0.0 copy-start.1
  95.9 0.1 mul.115
  96.0 0.7 copy-done.1
  96.7 0.1 reshape.48
  96.8 0.0 copy-start
  96.8 30.1 %all-reduce.4.cloned.1.call-done = f32[2,2,8192]{2,1,0:T(2,128)} async-done(((f32[2,2,8192]{2,1,0:T(2,128)}), f32[2,2,8192]{2,1,0:T(2,128)}) %all-reduce.4.cloned.1.call-update) | async-done | bytes 131088 | tf_op jit(solution)/shard_map/psum | solution.py:34
  126.9 0.0 copy-start.3
  126.9 1.7 multiply_reduce_fusion
  128.6 0.0 copy-done
  128.6 0.0 copy-start.2
  128.6 0.1 reshape.49
  128.6 22.0 %psum.15 = f32[]{:T(128)} all-reduce(f32[]{:T(128)} %multiply_reduce_fusion), channel_id=1, replica_groups=mesh['dp'=8,'outer'=4] {'dp'}, use_global_device_ids=true, to_apply=%region_3.0 | all-reduce | flops 1 | bytes 8 | tf_op jit(solution)/shard_map/psum | solution.py:35
  151.4 0.0 copy-done.3
  151.4 0.0 copy-done.2
  151.4 1.1 fusion.4
  152.5 0.1 mul.127
  152.6 0.3 fusion.3
  152.9 0.0 copy-start.7
  152.9 0.0 copy-start.6
  152.9 0.1 div.47
  153.0 0.5 copy-done.7
  153.5 0.1 div.48
  153.6 0.0 copy-done.6
  153.6 0.1 div.50
  153.7 0.1 div.51
  153.9 1.2 stack.2
  155.1 3.5 %all-to-all-start = ((bf16[8,2,2,8192]{3,2,1,0:T(2,128)(2,1)}), bf16[8,2,2,8192]{3,2,1,0:T(2,128)(2,1)S(1)}, u32[]{:S(2)}, u32[]{:S(2)}) async-start(bf16[8,2,2,8192]{3,2,1,0:T(2,128)(2,1)} %stack.2), calls=%async_computation | async-start | bytes 1048576 | tf_op jit(solution)/shard_map/all_to_all | solution.py:40
  158.6 1.0 divide_convert_fusion
  159.5 9.2 %all-to-all-done = bf16[8,2,2,8192]{3,2,1,0:T(2,128)(2,1)S(1)} async-done(((bf16[8,2,2,8192]{3,2,1,0:T(2,128)(2,1)}), bf16[8,2,2,8192]{3,2,1,0:T(2,128)(2,1)S(1)}, u32[]{:S(2)}, u32[]{:S(2)}) %all-to-all-start) | async-done | bytes 524320 | tf_op jit(solution)/shard_map/all_to_all | solution.py:40
  168.8 0.5 copy.12
  169.3 1.1 copy.13
  (1 shorter events, 0.0 us)
Async XLA Ops:
  7.2 85.4 %all-reduce.6.cloned.1.call-start = ((), (), s32[]{:S(2)}) async-start(), calls=%async_computation.2 | async-start | bytes 2097152
  9.4 117.5 %all-reduce.4.cloned.1.call-start = ((), (), s32[]{:S(2)}) async-start(), calls=%async_computation.1 | async-start | bytes 262144 | tf_op jit(solution)/shard_map/psum | solution.py:34
  9.4 0.7 copy-start.8
  94.3 0.7 copy-start.5
  95.1 0.7 copy-start.4
  95.9 0.8 copy-start.1
  96.8 31.8 %copy-start = (bf16[2,2,8192]{2,1,0:T(2,128)(2,1)S(1)}, bf16[2,2,8192]{2,1,0:T(2,128)(2,1)}, u32[]{:S(2)}) copy-start(bf16[2,2,8192]{2,1,0:T(2,128)(2,1)} %param.9) | copy-start | bytes 196612
  126.9 24.5 %copy-start.3 = (f32[2,2,8192]{2,1,0:T(2,128)S(1)}, f32[2,2,8192]{2,1,0:T(2,128)}, u32[]{:S(2)}) copy-start(f32[2,2,8192]{2,1,0:T(2,128)} %param.7) | copy-start | bytes 393220
  128.6 22.8 %copy-start.2 = (f32[2,2,8192]{2,1,0:T(2,128)S(1)}, f32[2,2,8192]{2,1,0:T(2,128)}, u32[]{:S(2)}) copy-start(f32[2,2,8192]{2,1,0:T(2,128)} %all-reduce.4.cloned.1.call-done) | copy-start | bytes 393220
  152.9 0.6 copy-start.7
  152.9 0.7 copy-start.6
  155.1 13.7 %all-to-all-start = ((bf16[8,2,2,8192]{3,2,1,0:T(2,128)(2,1)}), bf16[8,2,2,8192]{3,2,1,0:T(2,128)(2,1)S(1)}, u32[]{:S(2)}, u32[]{:S(2)}) async-start(bf16[8,2,2,8192]{3,2,1,0:T(2,128)(2,1)} %stack.2), calls=%async_computation | async-start | bytes 1048576 | tf_op jit(solution)/shard_map/all_to_all | solution.py:40
Sparse Core Ops, SparseCore 0:
  11.5 81.0 all-reduce.5
  95.5 31.3 all-reduce.3
